TPU v7x, 256 devices: a whole 4x4x8 slice. The times are simulated.
256 devices in a mesh: gx: 8 (over z), gy: 32 (over x, y, core).
Axes of the slice: x: 4, y: 4, z: 8, core: 2. Of those that a mesh axis runs over, the one named last changes fastest.
Arguments:
- permeability: float32 [3, 256, 65536], P(None, 'gx', 'gy'), may hold values from 0.03 to 1000, as said below
Outputs:
- fine_pressure: float32 [256, 65536], P('gx', 'gy')
- twin_pressure: float32 [128, 16384], P('gx', 'gy')
Inputs may be any that keep to these rules, and one draw needn't show every extreme that they name: `permeability`: positive conductivities; entry 0, 1, 2 of the first dimension is the conductivity along the grid's first, second, third dimension.
All inputs are finite; a program needn't handle non-finite values.
Results may differ from a plain program's by a relative error of at most 0.0003.
Values sent between devices are 32-bit elements; how exact they have to be, the bound alone decides.
A program may use at most 192 MiB of HBM per device.

v0:
```python
import jax
import jax.numpy as jnp
from jax import lax
from jax.sharding import PartitionSpec as P

EL = 32
ELZ = 16
MX = 4
MZ = 2
EZ = 2
PATCH_ITERS = 3
COARSE_ITERS = 2


def shifted(shard, axis, by):
    count = lax.axis_size(axis)
    return lax.ppermute(shard, axis, [(i, (i + by) % count) for i in range(count)])


def padded_2(cells, sides, width):
    for axis, dim in sides:
        count = lax.axis_size(axis)
        head = lax.slice_in_dim(cells, 0, width, axis=dim)
        tail = lax.slice_in_dim(cells, cells.shape[dim] - width, cells.shape[dim], axis=dim)
        cells = jnp.concatenate(
            [
                lax.ppermute(tail, axis, [(i, (i + 1) % count) for i in range(count)]),
                cells,
                lax.ppermute(head, axis, [((i + 1) % count, i) for i in range(count)]),
            ],
            axis=dim,
        )
    return cells


def harmonic(first, second, spacing):
    return spacing * 2.0 * first * second / (first + second)


def face_weights(conduct, width, spacing):
    weight_rows = harmonic(conduct[0][..., :-width], conduct[0][..., width:], spacing)
    weight_cols = harmonic(conduct[1][..., :-1], conduct[1][..., 1:], spacing)
    column = jnp.arange(weight_cols.shape[-1], dtype=jnp.int32) % width
    weight_cols = jnp.where(column == width - 1, jnp.zeros_like(weight_cols), weight_cols)
    weight_depth = harmonic(conduct[2][:, :-1], conduct[2][:, 1:], spacing)
    return (weight_rows, weight_cols, weight_depth)


def apply_operator(field, weights, width):
    weight_rows, weight_cols, weight_depth = weights
    flux = weight_rows * (field[..., :-width] - field[..., width:])
    result = jnp.pad(flux, ((0, 0), (0, 0), (0, 0), (0, width))) - jnp.pad(
        flux, ((0, 0), (0, 0), (0, 0), (width, 0))
    )
    flux = weight_cols * (field[..., :-1] - field[..., 1:])
    result = (
        result
        + jnp.pad(flux, ((0, 0), (0, 0), (0, 0), (0, 1)))
        - jnp.pad(flux, ((0, 0), (0, 0), (0, 0), (1, 0)))
    )
    flux = weight_depth * (field[:, :, :-1] - field[:, :, 1:])
    result = (
        result
        + jnp.pad(flux, ((0, 0), (0, 0), (0, 1), (0, 0)))
        - jnp.pad(flux, ((0, 0), (0, 0), (1, 0), (0, 0)))
    )
    return result


def interior_mask(depth, rows, width):
    level = jnp.arange(depth, dtype=jnp.int32)[:, None]
    cell = jnp.arange(rows * width, dtype=jnp.int32)[None, :]
    row_index = cell // width
    line_index = cell % width
    inside = (
        (level > 0)
        & (level < depth - 1)
        & (row_index > 0)
        & (row_index < rows - 1)
        & (line_index > 0)
        & (line_index < width - 1)
    )
    return inside.astype(jnp.float32)


def shape_functions(depth, rows, width, edge, edge_depth, margin, margin_depth):
    cell = jnp.arange(rows * width, dtype=jnp.int32)
    place_rows = ((cell // width).astype(jnp.float32) - margin + 0.5) / edge
    place_cols = ((cell % width).astype(jnp.float32) - margin + 0.5) / edge
    place_depth = (
        jnp.arange(depth, dtype=jnp.int32).astype(jnp.float32) - margin_depth + 0.5
    ) / edge_depth
    factors = []
    for basis in range(8):
        along_rows = place_rows if basis // 4 else 1.0 - place_rows
        along_cols = place_cols if basis // 2 % 2 else 1.0 - place_cols
        along_depth = place_depth if basis % 2 else 1.0 - place_depth
        factors.append(along_depth[:, None] * (along_rows * along_cols)[None, :])
    return jnp.stack(factors)[:, None]


def patch_fields(block, edge_depth, margin_depth):
    depth = edge_depth + 2 * margin_depth
    count = (block.shape[3] - 2 * margin_depth) // edge_depth
    pieces = [
        block[:, :, :, index * edge_depth : index * edge_depth + depth] for index in range(count)
    ]
    stacked = jnp.stack(pieces, axis=1)
    return jnp.transpose(stacked, (0, 1, 4, 2, 3)).reshape(
        3, count, depth, block.shape[1] * block.shape[2]
    )


def solve_column(block, edge, edge_depth, margin, margin_depth, spacing):
    rows = block.shape[1]
    width = block.shape[2]
    depth = edge_depth + 2 * margin_depth
    conduct = patch_fields(block, edge_depth, margin_depth)
    count = conduct.shape[1]
    weights = face_weights(conduct, width, spacing)
    inside = interior_mask(depth, rows, width)
    start = shape_functions(depth, rows, width, edge, edge_depth, margin, margin_depth)
    residual = -inside * apply_operator(start, weights, width)
    direction = residual
    norm_now = jnp.sum(residual * residual, axis=(2, 3), keepdims=True)
    update = jnp.zeros_like(residual)
    for step in range(PATCH_ITERS):
        image = inside * apply_operator(direction, weights, width)
        alpha = norm_now / jnp.sum(direction * image, axis=(2, 3), keepdims=True)
        update = update + alpha * direction
        residual = residual - alpha * image
        norm_next = jnp.sum(residual * residual, axis=(2, 3), keepdims=True)
        direction = residual + norm_next / norm_now * direction
        norm_now = norm_next
    solution = start + update
    local = solution.reshape(8, count, depth, rows, width)[
        :,
        :,
        margin_depth : margin_depth + edge_depth,
        margin : margin + edge,
        margin : margin + edge,
    ]
    local = local.reshape(8, count, edge_depth, edge * edge)
    element_conduct = conduct.reshape(3, count, depth, rows, width)[
        :,
        :,
        margin_depth : margin_depth + edge_depth,
        margin : margin + edge,
        margin : margin + edge,
    ]
    element_conduct = element_conduct.reshape(3, count, edge_depth, edge * edge)
    inner_rows, inner_cols, inner_depth = face_weights(element_conduct, edge, spacing)
    jump = local[..., :-edge] - local[..., edge:]
    stiffness = jnp.einsum(
        "aezn,bezn->eab", jump * inner_rows, jump, precision=lax.Precision.HIGHEST
    )
    jump = local[..., :-1] - local[..., 1:]
    stiffness = stiffness + jnp.einsum(
        "aezn,bezn->eab", jump * inner_cols, jump, precision=lax.Precision.HIGHEST
    )
    jump = local[:, :, :-1] - local[:, :, 1:]
    stiffness = stiffness + jnp.einsum(
        "aezn,bezn->eab", jump * inner_depth, jump, precision=lax.Precision.HIGHEST
    )
    return (local, stiffness)


def coarsen(block):
    comps, rows, width, depth = block.shape
    grouped = block.reshape(comps, rows // 2, 2, width // 2, 2, depth // 2, 2)
    return 0.125 * jnp.sum(grouped, axis=(2, 4, 6))


def corner_stack(corner_first, corner_rows, corner_cols, corner_both, count):
    table = [[corner_first, corner_cols], [corner_rows, corner_both]]
    values = []
    for basis in range(8):
        lift = basis % 2
        values.append(table[basis // 4][basis // 2 % 2][..., lift : lift + count])
    return jnp.stack(values, axis=-1)


def spread(values):
    parts = [[None, None], [None, None]]
    for basis in range(8):
        lift = basis % 2
        widths = [(0, 0)] * (values.ndim - 2) + [(lift, 1 - lift)]
        padded = jnp.pad(values[..., basis], widths)
        first = basis // 4
        second = basis // 2 % 2
        if parts[first][second] is None:
            parts[first][second] = padded
        else:
            parts[first][second] = parts[first][second] + padded
    return parts


def pressure_tile(local, weights, edge):
    combined = jnp.sum(jnp.transpose(weights)[:, :, None, None] * local, axis=0)
    count = combined.shape[0]
    depth = combined.shape[1]
    return jnp.transpose(combined.reshape(count, depth, edge, edge), (2, 3, 0, 1)).reshape(
        edge, edge, count * depth
    )


def neighbours(nodes):
    next_rows = shifted(nodes, "gx", -1)
    fetched = shifted(jnp.stack([nodes[:, 0], next_rows[:, 0]]), "gy", -1)
    next_cols = jnp.concatenate([nodes[:, 1:], fetched[0][:, None]], axis=1)
    next_both = jnp.concatenate([next_rows[:, 1:], fetched[1][:, None]], axis=1)
    return (next_rows, next_cols, next_both)


def local_operator(stiffness, nodes, count):
    next_rows, next_cols, next_both = neighbours(nodes)
    element = corner_stack(nodes, next_rows, next_cols, next_both, count)
    local = jnp.einsum("lckab,lckb->lcka", stiffness, element, precision=lax.Precision.HIGHEST)
    parts = spread(local)
    col_part = parts[0][1]
    both_part = parts[1][1]
    returned = shifted(jnp.stack([col_part[:, -1], both_part[:, -1]]), "gy", 1)
    moved_cols = jnp.concatenate([returned[0][:, None], col_part[:, :-1]], axis=1)
    moved_both = jnp.concatenate([returned[1][:, None], both_part[:, :-1]], axis=1)
    across = shifted(parts[1][0] + moved_both, "gx", 1)
    return parts[0][0] + moved_cols + across


def squares(residual):
    return lax.psum(jnp.sum(residual * residual, axis=(1, 2), keepdims=True), ("gx", "gy"))


def spread_solve(stiffness, columns, count):
    level = jnp.arange(count + 1, dtype=jnp.int32)
    inside = ((level > 0) & (level < count)).astype(jnp.float32)
    boundary = jnp.broadcast_to((level == 0).astype(jnp.float32), (2, columns, count + 1))
    source = -inside * local_operator(stiffness, boundary, count)
    update = jnp.zeros_like(source)
    residual = source
    direction = source
    norm_now = squares(residual)
    for step in range(COARSE_ITERS):
        image = inside * local_operator(stiffness, direction, count)
        alpha = norm_now / lax.psum(
            jnp.sum(direction * image, axis=(1, 2), keepdims=True), ("gx", "gy")
        )
        update = update + alpha * direction
        residual = residual - alpha * image
        norm_next = squares(residual)
        direction = residual + norm_next / norm_now * direction
        norm_now = norm_next
    return boundary + update


def shards(permeability):
    depth_total = ELZ * EZ
    shaped = permeability.reshape(
        3, permeability.shape[1], permeability.shape[2] // depth_total, depth_total
    )
    rimmed = padded_2(shaped, (("gx", 1), ("gy", 2)), MX)
    half_edge = EL // 2
    columns = shaped.shape[2] // EL

    def column_work(offset):
        block = lax.dynamic_slice_in_dim(rimmed, offset, EL + 2 * MX, 2)
        fine_block = jnp.pad(block, ((0, 0), (0, 0), (0, 0), (MZ, MZ)), mode="edge")
        twin_block = coarsen(fine_block)
        fine_local, fine_stiff = solve_column(fine_block, EL, ELZ, MX, MZ, 1.0)
        twin_local, twin_stiff = solve_column(
            twin_block, half_edge, ELZ // 2, MX // 2, MZ // 2, 2.0
        )
        return (fine_local, fine_stiff, twin_local, twin_stiff)

    offsets = jnp.arange(columns, dtype=jnp.int32) * EL
    fine_local, fine_stiff, twin_local, twin_stiff = lax.map(column_work, offsets)
    stiffness = jnp.stack([fine_stiff, twin_stiff])
    count = stiffness.shape[2]
    corner_first = spread_solve(stiffness, columns, count)
    corner_rows, corner_cols, corner_both = neighbours(corner_first)
    weights = corner_stack(corner_first, corner_rows, corner_cols, corner_both, count)
    fine_tiles = [
        pressure_tile(fine_local[column], weights[0, column], EL) for column in range(columns)
    ]
    twin_tiles = [
        pressure_tile(twin_local[column], weights[1, column], half_edge)
        for column in range(columns)
    ]
    fine_pressure = jnp.concatenate(fine_tiles, axis=1)
    twin_pressure = jnp.concatenate(twin_tiles, axis=1)
    return (fine_pressure.reshape(EL, -1), twin_pressure.reshape(half_edge, -1))


def solution(mesh):
    placed = (P(None, "gx", "gy"),)
    return jax.shard_map(
        shards,
        mesh=mesh,
        in_specs=placed,
        out_specs=(P("gx", "gy"), P("gx", "gy")),
        check_vma=False,
    )
```

profile of v0, /device:TPU:1, one launch (start us, length us, event | category | flops | bytes accessed | tf_op | source)
XLA Modules:
  0.0 635.2 jit_solution(149568154038995864)
XLA Ops:
  0.6 2.1 reshape.1460
  3.7 2.5 collective-permute-start
  6.1 3.9 collective-permute-start.1
  13.8 4.4 collective-permute-done.4
  21.2 2.5 collective-permute-done.5
  25.7 1.9 copy-done.12
  27.6 2.6 collective-permute-start.3
  32.8 2.7 copy.335
  35.6 2.1 copy.336
  37.6 2.0 copy.334
  39.7 4.5 pad_maximum_fusion.3
  44.2 299.3 %while.21 = (s32[]{:T(128)}, f32[2,8,2,16,1024]{4,1,3,2,0:T(8,128)}, f32[2,2,8,8]{3,2,1,0:T(8,128)}, f32[2,8,2,8,256]{4,1,3,2,0:T(8,128)}, f32[2,2,8,8]{3,2,1,0:...) while((s32[]{:T(128)}, ...), condition=%wide.region_14.15_spmd, body=%wide.region_0.14_spmd.sunk | while | flops 130577320 | bytes 255059728 | solution.py:275
  45.1 1.7 stack.282
  50.3 2.1 constant_dynamic-slice_fusion.2
  62.3 2.2 reshape.1501
  66.1 1.6 broadcast_multiply_fusion.34
  69.1 2.2 reshape.1502
  88.3 2.0 add_add_fusion.5
  90.3 5.9 reshape.1503
  96.2 5.7 slice.2293
  102.0 3.7 broadcast_in_dim.249
  106.8 3.9 reshape.1504
  110.7 2.9 fusion.260
  113.6 1.9 squeeze.279
  116.6 2.3 fusion.261
  118.9 1.9 squeeze.280
  121.9 2.5 fusion.262
  126.4 3.0 fusion.264
  131.4 26.2 %reshape.1505 = f32[3,20,2,20,2,18,2]{4,3,2,1,6,5,0:T(8,128)} reshape(f32[3,40,40,36]{2,1,3,0:T(8,128)} %pad_maximum_fusion.26) | data formatting | bytes 1382400 | tf_op jit(solution)/shard_map/while/body/eval_jaxpr/reshape | solution.py:170
  157.7 19.5 %reduce_sum.329 = f32[3,20,20,18]{2,1,3,0:T(8,128)S(1)} reduce(f32[3,20,2,20,2,18,2]{4,3,2,1,6,5,0:T(8,128)} %reshape.1505, f32[]{:T(128)} %constant.340.clone.31..sunk), dimensions={2,4,6}, to_apply=%region_7.7 | reduce | flops 151200 | bytes 777604 | tf_op jit(solution)/shard_map/while/body/eval_jaxpr/reduce_sum | solution.py:171
  182.1 1.9 reshape.1506
  184.0 1.8 slice.2294
  190.5 1.7 stack.282
  195.8 2.1 constant_dynamic-slice_fusion.2
  207.8 2.2 reshape.1501
  214.6 2.2 reshape.1502
  233.5 2.0 add_add_fusion.5
  235.5 5.9 reshape.1503
  241.5 5.7 slice.2293
  247.2 3.7 broadcast_in_dim.249
  252.0 4.0 reshape.1504
  256.0 2.9 fusion.260
  258.9 1.9 squeeze.279
  261.8 2.3 fusion.261
  264.1 1.9 squeeze.280
  267.2 2.5 fusion.262
  271.7 3.0 fusion.264
  276.7 26.2 %reshape.1505 = f32[3,20,2,20,2,18,2]{4,3,2,1,6,5,0:T(8,128)} reshape(f32[3,40,40,36]{2,1,3,0:T(8,128)} %pad_maximum_fusion.26) | data formatting | bytes 1382400 | tf_op jit(solution)/shard_map/while/body/eval_jaxpr/reshape | solution.py:170
  302.9 19.7 %reduce_sum.329 = f32[3,20,20,18]{2,1,3,0:T(8,128)S(1)} reduce(f32[3,20,2,20,2,18,2]{4,3,2,1,6,5,0:T(8,128)} %reshape.1505, f32[]{:T(128)} %constant.340.clone.31..sunk), dimensions={2,4,6}, to_apply=%region_7.7 | reduce | flops 151200 | bytes 777604 | tf_op jit(solution)/shard_map/while/body/eval_jaxpr/reduce_sum | solution.py:171
  327.6 1.9 reshape.1506
  329.5 1.8 slice.2294
  344.9 7.2 %collective-permute-done.6 = f32[2,2,3]{2,1,0:T(2,128)S(1)} collective-permute-done((f32[2,2,3]{2,1,0:T(2,128)S(1)}, f32[2,2,3]{2,1,0:T(2,128)S(1)}, u32[]{:S(2)}, u32[]{:S(2)}) %collective-permute-start.6) | collective-permute-done | bytes 80 | tf_op jit(solution)/shard_map/ppermute | solution.py:17
  352.2 4.6 collective-permute-done.7
  360.1 7.4 %collective-permute-start.9 = (f32[2,2,3]{2,1,0:T(2,128)S(1)}, f32[2,2,3]{2,1,0:T(2,128)S(1)}, u32[]{:S(2)}, u32[]{:S(2)}) collective-permute-start(f32[2,2,3]{2,1,0:T(2,128)S(1)} %pad_maximum_fusion.20), channel_id=1, source_target_pairs={{0,31},{1,0},{2,1},{3,2},{4,3},{5,4},{6,5},{7,6},{8,7},{9,8},{10,9... | collective-permute-start | bytes 152 | tf_op jit(solution)/shard_map/ppermute | solution.py:17
  371.6 4.2 collective-permute-done.11
  376.6 77.9 %all-reduce.72 = (f32[2,1,1]{0,2,1:T(1,128)S(1)}, f32[2,1,1]{0,2,1:T(1,128)S(1)}) all-reduce(f32[2,1,1]{0,2,1:T(1,128)S(1)} %bitcast.449, f32[2,1,1]{0,2,1:T(1,128)S(1)} %bitcast.448), channel_id=1, replica_groups=mesh['gx'=8,'gy'=32] {'gx','gy'}, use_global_device_ids=true, to_apply=%region_16.17 | all-reduce | flops 4 | bytes 32 | tf_op jit(solution)/shard_map/psum | solution.py:230
  454.7 73.6 %psum.30 = f32[2,1,1]{0,2,1:T(1,128)S(1)} all-reduce(f32[2,1,1]{0,2,1:T(1,128)S(1)} %bitcast.451), channel_id=1, replica_groups=mesh['gx'=8,'gy'=32] {'gx','gy'}, use_global_device_ids=true, to_apply=%region_20.21 | all-reduce | flops 2 | bytes 16 | tf_op jit(solution)/shard_map/psum | solution.py:230
  528.5 1.7 collective-permute-start.12
  533.1 2.0 collective-permute-done.13
  538.3 1.7 collective-permute-start.15
  540.0 2.5 collective-permute-done.15
  543.3 77.1 %psum.31 = f32[2,1,1]{0,2,1:T(1,128)S(1)} all-reduce(f32[2,1,1]{0,2,1:T(1,128)S(1)} %bitcast.450), channel_id=1, replica_groups=mesh['gx'=8,'gy'=32] {'gx','gy'}, use_global_device_ids=true, to_apply=%region_22.23 | all-reduce | flops 2 | bytes 16 | tf_op jit(solution)/shard_map/psum | solution.py:244
  623.9 1.8 collective-permute-start.17
  628.3 2.3 fusion.116
  (519 shorter events, 135.0 us)
Async XLA Ops:
  3.7 20.6 %collective-permute-start = (f32[3,4,64,32]{3,2,1,0:T(8,128)}, f32[3,4,64,32]{3,2,1,0:T(8,128)}, u32[]{:S(2)}, u32[]{:S(2)}) collective-permute-start(f32[3,4,64,32]{3,2,1,0:T(8,128)} %get-tuple-element.370), channel_id=1, source_target_pairs={{0,32},{32,64},{64,96},{96,128},{128,160},{160,192},{192,224},{224... | collective-permute-start | bytes 294920 | tf_op jit(solution)/shard_map/ppermute | solution.py:27
  6.1 19.5 %collective-permute-start.1 = (f32[3,4,64,32]{3,2,1,0:T(8,128)}, f32[3,4,64,32]{3,2,1,0:T(8,128)S(1)}, u32[]{:S(2)}, u32[]{:S(2)}) collective-permute-start(f32[3,4,64,32]{3,2,1,0:T(8,128)} %get-tuple-element.369), channel_id=1, source_target_pairs={{32,0},{64,32},{96,64},{128,96},{160,128},{192,160},{224,192},{0,2... | collective-permute-start | bytes 294920 | tf_op jit(solution)/shard_map/ppermute | solution.py:29
  10.1 20.1 %copy-start.18 = (f32[3]{0:T(128)}, f32[3]{0:T(128)S(1)}, u32[]{:S(2)}) copy-start(f32[3]{0:T(128)S(1)} %compare_convert_fusion) | copy-start | bytes 40
  10.1 8.1 %collective-permute-start.4 = (f32[2,2,3]{2,0,1:T(2,128)S(1)}, f32[2,2,3]{2,0,1:T(2,128)S(1)}, u32[]{:S(2)}, u32[]{:S(2)}) collective-permute-start(f32[2,2,3]{2,0,1:T(2,128)S(1)} %broadcast_in_dim.227), channel_id=1, source_target_pairs={{0,224},{32,0},{64,32},{96,64},{128,96},{160,128},{192,160},{224,1... | collective-permute-start | bytes 152 | tf_op jit(solution)/shard_map/ppermute | solution.py:17
  19.3 4.3 collective-permute-start.5
  25.4 4.9 copy-start.19
  25.6 1.9 copy-start.12
  27.6 7.9 %collective-permute-start.3 = (f32[3,40,4,32]{3,2,1,0:T(4,128)S(1)}, f32[3,40,4,32]{3,2,1,0:T(4,128)S(1)}, u32[]{:S(2)}, u32[]{:S(2)}) collective-permute-start(f32[3,40,4,32]{3,2,1,0:T(4,128)S(1)} %get-tuple-element.368), channel_id=1, source_target_pairs={{1,0},{2,1},{3,2},{4,3},{5,4},{6,5},{7,6},{8,7},{9,8},{10,9},{11,1... | collective-permute-start | bytes 184328 | tf_op jit(solution)/shard_map/ppermute | solution.py:29
  30.2 7.4 %collective-permute-start.2 = (f32[3,40,4,32]{3,2,1,0:T(4,128)S(1)}, f32[3,40,4,32]{3,2,1,0:T(4,128)S(1)}, u32[]{:S(2)}, u32[]{:S(2)}) collective-permute-start(f32[3,40,4,32]{3,2,1,0:T(4,128)S(1)} %get-tuple-element.367), channel_id=1, source_target_pairs={{0,1},{1,2},{2,3},{3,4},{4,5},{5,6},{6,7},{7,8},{8,9},{9,10},{10,1... | collective-permute-start | bytes 184328 | tf_op jit(solution)/shard_map/ppermute | solution.py:27
  39.7 4.5 copy-start.20
  53.6 0.6 copy-start.8
  53.7 0.7 copy-start.10
  54.5 2.3 copy-start
  58.3 1.2 copy-start.7
  64.5 1.6 copy-start.5
  66.1 3.0 copy-start.3
  71.3 1.6 copy-start.6
  72.8 1.6 copy-start.1
  72.8 2.2 copy-start.2
  76.3 1.0 copy-start.4
  125.3 4.6 copy-start.9
  125.3 4.6 copy-start.11
  184.0 2.2 copy-start.13
  185.8 2.6 copy-start.16
  186.3 3.2 copy-start.21
  186.3 2.6 copy-start.14
  188.9 0.6 copy-start.17
  199.1 0.6 copy-start.8
  199.1 0.7 copy-start.10
  199.9 2.3 copy-start
  203.7 1.2 copy-start.7
  210.0 1.6 copy-start.5
  211.6 3.0 copy-start.3
  216.7 1.6 copy-start.6
  218.3 1.6 copy-start.1
  218.3 2.2 copy-start.2
  221.8 1.0 copy-start.4
  270.5 4.6 copy-start.9
  270.5 4.6 copy-start.11
  329.5 2.2 copy-start.13
  331.3 2.6 copy-start.16
  331.8 3.2 copy-start.21
  331.8 2.6 copy-start.14
  334.3 0.6 copy-start.17
  344.8 7.3 %collective-permute-start.6 = (f32[2,2,3]{2,1,0:T(2,128)S(1)}, f32[2,2,3]{2,1,0:T(2,128)S(1)}, u32[]{:S(2)}, u32[]{:S(2)}) collective-permute-start(f32[2,2,3]{2,1,0:T(2,128)S(1)} %pad_maximum_fusion.19), channel_id=1, source_target_pairs={{0,1},{1,2},{2,3},{3,4},{4,5},{5,6},{6,7},{7,8},{8,9},{9,10},{10,1... | collective-permute-start | bytes 152 | tf_op jit(solution)/shard_map/ppermute | solution.py:17
  352.2 4.6 collective-permute-start.7
  357.6 2.4 collective-permute-start.8
  360.1 8.2 %collective-permute-start.9 = (f32[2,2,3]{2,1,0:T(2,128)S(1)}, f32[2,2,3]{2,1,0:T(2,128)S(1)}, u32[]{:S(2)}, u32[]{:S(2)}) collective-permute-start(f32[2,2,3]{2,1,0:T(2,128)S(1)} %pad_maximum_fusion.20), channel_id=1, source_target_pairs={{0,31},{1,0},{2,1},{3,2},{4,3},{5,4},{6,5},{7,6},{8,7},{9,8},{10,9... | collective-permute-start | bytes 152 | tf_op jit(solution)/shard_map/ppermute | solution.py:17
  370.2 1.2 collective-permute-start.10
  371.5 4.2 collective-permute-start.11
  528.5 2.7 collective-permute-start.12
  531.2 3.9 collective-permute-start.13
  537.0 1.2 collective-permute-start.14
  538.3 4.2 collective-permute-start.15
  621.2 2.7 collective-permute-start.16
  623.9 3.7 collective-permute-start.17
  631.5 1.8 copy-start.15
where the time goes:
time: 646 us; the launch traced here: 635 us
  blocking collectives  229 us (35%)
  local copies, waits for them, and re-layouts  188 us (29%)
  other arithmetic  118 us (18%)
  waiting for transfers between devices  34.7 us (5%)
  starting transfers between devices  28.8 us (4%)
  matrix products  20.8 us (3%)
  loops' own time  14.6 us (2%)
    psum x2, blocking collectives, squares(): lax.psum(jnp.sum(residual * residual, axis=(1, 2), keepdims=True), ('gx',...  152 us
    psum x1, blocking collectives, spread_solve(): lax.psum(jnp.sum(direction * image, axis=(1, 2), keepdims=True), ('gx', '...  77.1 us
    reshape x2, local copies, waits for them, and re-layouts, coarsen(): grouped = block.reshape(comps, rows // 2, 2, width // 2, 2, depth // 2, 2)  52.5 us
    reduce_sum x2, other arithmetic, coarsen(): return 0.125 * jnp.sum(grouped, axis=(2, 4, 6))  39.3 us
    ppermute x14, waiting for transfers between devices, shifted(): lax.ppermute(shard, axis, [(i, (i + by) % count) for i in range(count)])  34.7 us
    ppermute x14, starting transfers between devices, shifted(): lax.ppermute(shard, axis, [(i, (i + by) % count) for i in range(count)])  19.8 us
    reshape x4, local copies, waits for them, and re-layouts, solve_column(): solution.reshape(8, count, depth, rows, width)  15.7 us
    slice x4, local copies, waits for them, and re-layouts, solve_column(): solution.reshape(8, count, depth, rows, width)  15 us
  transfers between devices with their start and end apart: 18, of which 14 were waited for; matrix products, arithmetic and copies ran while one was open for 2% of the time, Pallas kernels for 0%

commit v1 on v0

--- a/solution.py
+++ b/solution.py
@@ -241,8 +241,14 @@
     norm_now = squares(residual)
     for step in range(COARSE_ITERS):
         image = inside * local_operator(stiffness, direction, count)
-        alpha = norm_now / lax.psum(
-            jnp.sum(direction * image, axis=(1, 2), keepdims=True), ("gx", "gy")
+
+        def choose_the_rounds(unit, which_axis, axis_name):
+            for b in (which_axis, axis_name):
+                unit = lax.psum(unit, b)
+            return unit
+
+        alpha = norm_now / choose_the_rounds(
+            jnp.sum(direction * image, axis=(1, 2), keepdims=True), "gy", axis_name="gx"
         )
         update = update + alpha * direction
         residual = residual - alpha * image

time: 646 us -> 729 us (1.13)
  blocking collectives: 229 us -> 309 us
    psum x1 -> x4, blocking collectives: 77.1 us -> 160 us  [choose_the_rounds(): unit = lax.psum(unit, b)]
where the time goes in v1:
time: 729 us; the launch traced here: 718 us
  blocking collectives  309 us (42%)
  local copies, waits for them, and re-layouts  187 us (26%)
  other arithmetic  119 us (16%)
  waiting for transfers between devices  34.1 us (5%)
  starting transfers between devices  31.5 us (4%)
  matrix products  20.8 us (3%)
  loops' own time  14.7 us (2%)
    psum x4, blocking collectives, choose_the_rounds(): unit = lax.psum(unit, b)  160 us
    psum x2, blocking collectives, squares(): lax.psum(jnp.sum(residual * residual, axis=(1, 2), keepdims=True), ('gx',...  150 us
    reshape x2, local copies, waits for them, and re-layouts, coarsen(): grouped = block.reshape(comps, rows // 2, 2, width // 2, 2, depth // 2, 2)  52.3 us
    reduce_sum x2, other arithmetic, coarsen(): return 0.125 * jnp.sum(grouped, axis=(2, 4, 6))  39.3 us
    ppermute x14, waiting for transfers between devices, shifted(): lax.ppermute(shard, axis, [(i, (i + by) % count) for i in range(count)])  34.1 us
    ppermute x14, starting transfers between devices, shifted(): lax.ppermute(shard, axis, [(i, (i + by) % count) for i in range(count)])  22.5 us
    reshape x4, local copies, waits for them, and re-layouts, solve_column(): solution.reshape(8, count, depth, rows, width)  15.6 us
    slice x4, local copies, waits for them, and re-layouts, solve_column(): solution.reshape(8, count, depth, rows, width)  15 us
  transfers between devices with their start and end apart: 18, of which 14 were waited for; matrix products, arithmetic and copies ran while one was open for 2% of the time, Pallas kernels for 0%

profile of v1, /device:TPU:1, one launch (start us, length us, event | category | flops | bytes accessed | tf_op | source)
XLA Modules:
  0.0 717.8 jit_solution(9210242526984584936)
XLA Ops:
  0.6 2.1 reshape.1460
  3.7 2.5 collective-permute-start
  6.1 3.9 collective-permute-start.1
  13.8 4.4 collective-permute-done.4
  21.2 2.5 collective-permute-done.5
  25.6 1.9 copy-done.12
  27.6 2.6 collective-permute-start.3
  32.9 2.7 copy.335
  35.6 2.1 copy.336
  37.7 2.1 copy.334
  39.8 4.5 pad_maximum_fusion.3
  44.3 299.0 %while.21 = (s32[]{:T(128)}, f32[2,8,2,16,1024]{4,1,3,2,0:T(8,128)}, f32[2,2,8,8]{3,2,1,0:T(8,128)}, f32[2,8,2,8,256]{4,1,3,2,0:T(8,128)}, f32[2,2,8,8]{3,2,1,0:...) while((s32[]{:T(128)}, ...), condition=%wide.region_14.15_spmd, body=%wide.region_0.14_spmd.sunk | while | flops 130577320 | bytes 255059728 | solution.py:281
  50.4 2.1 constant_dynamic-slice_fusion.2
  62.4 2.1 reshape.1501
  69.1 2.1 reshape.1502
  88.3 2.0 add_add_fusion.5
  90.3 5.9 reshape.1503
  96.2 5.7 slice.2293
  101.9 3.7 broadcast_in_dim.249
  106.7 3.9 reshape.1504
  110.6 2.9 fusion.260
  113.6 1.9 squeeze.279
  116.5 2.3 fusion.261
  118.8 1.9 squeeze.280
  121.8 2.5 fusion.262
  126.3 3.0 fusion.264
  131.4 26.2 %reshape.1505 = f32[3,20,2,20,2,18,2]{4,3,2,1,6,5,0:T(8,128)} reshape(f32[3,40,40,36]{2,1,3,0:T(8,128)} %pad_maximum_fusion.26) | data formatting | bytes 1382400 | tf_op jit(solution)/shard_map/while/body/eval_jaxpr/reshape | solution.py:170
  157.6 19.5 %reduce_sum.329 = f32[3,20,20,18]{2,1,3,0:T(8,128)S(1)} reduce(f32[3,20,2,20,2,18,2]{4,3,2,1,6,5,0:T(8,128)} %reshape.1505, f32[]{:T(128)} %constant.340.clone.31..sunk), dimensions={2,4,6}, to_apply=%region_7.7 | reduce | flops 151200 | bytes 777604 | tf_op jit(solution)/shard_map/while/body/eval_jaxpr/reduce_sum | solution.py:171
  182.0 1.9 reshape.1506
  184.0 1.8 slice.2294
  195.7 2.1 constant_dynamic-slice_fusion.2
  207.6 2.1 reshape.1501
  214.4 2.1 reshape.1502
  233.3 2.0 add_add_fusion.5
  235.4 5.9 reshape.1503
  241.3 5.7 slice.2293
  247.0 3.7 broadcast_in_dim.249
  251.8 4.0 reshape.1504
  255.8 2.9 fusion.260
  258.7 1.9 squeeze.279
  261.6 2.3 fusion.261
  263.9 1.9 squeeze.280
  267.0 2.5 fusion.262
  271.5 3.0 fusion.264
  276.5 26.2 %reshape.1505 = f32[3,20,2,20,2,18,2]{4,3,2,1,6,5,0:T(8,128)} reshape(f32[3,40,40,36]{2,1,3,0:T(8,128)} %pad_maximum_fusion.26) | data formatting | bytes 1382400 | tf_op jit(solution)/shard_map/while/body/eval_jaxpr/reshape | solution.py:170
  302.7 19.7 %reduce_sum.329 = f32[3,20,20,18]{2,1,3,0:T(8,128)S(1)} reduce(f32[3,20,2,20,2,18,2]{4,3,2,1,6,5,0:T(8,128)} %reshape.1505, f32[]{:T(128)} %constant.340.clone.31..sunk), dimensions={2,4,6}, to_apply=%region_7.7 | reduce | flops 151200 | bytes 777604 | tf_op jit(solution)/shard_map/while/body/eval_jaxpr/reduce_sum | solution.py:171
  327.4 1.9 reshape.1506
  329.3 1.8 slice.2294
  344.6 7.2 %collective-permute-done.6 = f32[2,2,3]{2,1,0:T(2,128)S(1)} collective-permute-done((f32[2,2,3]{2,1,0:T(2,128)S(1)}, f32[2,2,3]{2,1,0:T(2,128)S(1)}, u32[]{:S(2)}, u32[]{:S(2)}) %collective-permute-start.6) | collective-permute-done | bytes 80 | tf_op jit(solution)/shard_map/ppermute | solution.py:17
  351.9 4.6 collective-permute-done.7
  359.8 7.4 %collective-permute-start.9 = (f32[2,2,3]{2,1,0:T(2,128)S(1)}, f32[2,2,3]{2,1,0:T(2,128)S(1)}, u32[]{:S(2)}, u32[]{:S(2)}) collective-permute-start(f32[2,2,3]{2,1,0:T(2,128)S(1)} %pad_maximum_fusion.20), channel_id=1, source_target_pairs={{0,31},{1,0},{2,1},{3,2},{4,3},{5,4},{6,5},{7,6},{8,7},{9,8},{10,9... | collective-permute-start | bytes 152 | tf_op jit(solution)/shard_map/ppermute | solution.py:17
  371.2 4.2 collective-permute-done.11
  376.3 68.3 %psum.43 = f32[2,1,1]{0,2,1:T(1,128)S(1)} all-reduce(f32[2,1,1]{0,2,1:T(1,128)S(1)} %bitcast.449), channel_id=1, replica_groups=mesh['gx'=8,'gy'=32] {'gy'}, use_global_device_ids=true, to_apply=%region_18.19 | all-reduce | flops 2 | bytes 16 | tf_op jit(solution)/shard_map/psum | solution.py:247
  444.6 73.9 %psum.42 = f32[2,1,1]{0,2,1:T(1,128)S(1)} all-reduce(f32[2,1,1]{0,2,1:T(1,128)S(1)} %bitcast.448), channel_id=1, replica_groups=mesh['gx'=8,'gy'=32] {'gx','gy'}, use_global_device_ids=true, to_apply=%region_16.17 | all-reduce | flops 2 | bytes 16 | tf_op jit(solution)/shard_map/psum | solution.py:230
  518.5 11.6 %psum.44 = f32[2,1,1]{0,2,1:T(1,128)S(1)} all-reduce(f32[2,1,1]{0,2,1:T(1,128)S(1)} %psum.43), channel_id=1, replica_groups=mesh['gx'=8,'gy'=32] {'gx'}, use_global_device_ids=true, to_apply=%region_19.20 | all-reduce | flops 2 | bytes 16 | tf_op jit(solution)/shard_map/psum | solution.py:247
  530.2 75.7 %psum.45 = f32[2,1,1]{0,2,1:T(1,128)S(1)} all-reduce(f32[2,1,1]{0,2,1:T(1,128)S(1)} %bitcast.451), channel_id=1, replica_groups=mesh['gx'=8,'gy'=32] {'gx','gy'}, use_global_device_ids=true, to_apply=%region_21.22 | all-reduce | flops 2 | bytes 16 | tf_op jit(solution)/shard_map/psum | solution.py:230
  606.1 1.8 collective-permute-start.12
  615.2 1.8 collective-permute-start.15
  617.0 2.5 collective-permute-done.15
  620.3 67.6 %psum.46 = f32[2,1,1]{0,2,1:T(1,128)S(1)} all-reduce(f32[2,1,1]{0,2,1:T(1,128)S(1)} %bitcast.450), channel_id=1, replica_groups=mesh['gx'=8,'gy'=32] {'gy'}, use_global_device_ids=true, to_apply=%region_23.24 | all-reduce | flops 2 | bytes 16 | tf_op jit(solution)/shard_map/psum | solution.py:247
  687.9 12.3 %psum.47 = f32[2,1,1]{0,2,1:T(1,128)S(1)} all-reduce(f32[2,1,1]{0,2,1:T(1,128)S(1)} %psum.46), channel_id=1, replica_groups=mesh['gx'=8,'gy'=32] {'gx'}, use_global_device_ids=true, to_apply=%region_24.25 | all-reduce | flops 2 | bytes 16 | tf_op jit(solution)/shard_map/psum | solution.py:247
  701.4 2.4 collective-permute-done.16
  703.8 5.5 collective-permute-start.17
  710.9 2.3 fusion.116
  (522 shorter events, 137.8 us)
Async XLA Ops:
  3.7 20.6 %collective-permute-start = (f32[3,4,64,32]{3,2,1,0:T(8,128)}, f32[3,4,64,32]{3,2,1,0:T(8,128)}, u32[]{:S(2)}, u32[]{:S(2)}) collective-permute-start(f32[3,4,64,32]{3,2,1,0:T(8,128)} %get-tuple-element.368), channel_id=1, source_target_pairs={{0,32},{32,64},{64,96},{96,128},{128,160},{160,192},{192,224},{224... | collective-permute-start | bytes 294920 | tf_op jit(solution)/shard_map/ppermute | solution.py:27
  6.1 19.4 %collective-permute-start.1 = (f32[3,4,64,32]{3,2,1,0:T(8,128)}, f32[3,4,64,32]{3,2,1,0:T(8,128)S(1)}, u32[]{:S(2)}, u32[]{:S(2)}) collective-permute-start(f32[3,4,64,32]{3,2,1,0:T(8,128)} %get-tuple-element.367), channel_id=1, source_target_pairs={{32,0},{64,32},{96,64},{128,96},{160,128},{192,160},{224,192},{0,2... | collective-permute-start | bytes 294920 | tf_op jit(solution)/shard_map/ppermute | solution.py:29
  10.1 20.1 %copy-start.18 = (f32[3]{0:T(128)}, f32[3]{0:T(128)S(1)}, u32[]{:S(2)}) copy-start(f32[3]{0:T(128)S(1)} %compare_convert_fusion) | copy-start | bytes 40
  10.1 8.1 %collective-permute-start.4 = (f32[2,2,3]{2,0,1:T(2,128)S(1)}, f32[2,2,3]{2,0,1:T(2,128)S(1)}, u32[]{:S(2)}, u32[]{:S(2)}) collective-permute-start(f32[2,2,3]{2,0,1:T(2,128)S(1)} %broadcast_in_dim.227), channel_id=1, source_target_pairs={{0,224},{32,0},{64,32},{96,64},{128,96},{160,128},{192,160},{224,1... | collective-permute-start | bytes 152 | tf_op jit(solution)/shard_map/ppermute | solution.py:17
  19.3 4.3 collective-permute-start.5
  25.3 4.9 copy-start.19
  25.6 1.9 copy-start.12
  27.6 8.0 %collective-permute-start.3 = (f32[3,40,4,32]{3,2,1,0:T(4,128)S(1)}, f32[3,40,4,32]{3,2,1,0:T(4,128)S(1)}, u32[]{:S(2)}, u32[]{:S(2)}) collective-permute-start(f32[3,40,4,32]{3,2,1,0:T(4,128)S(1)} %get-tuple-element.366), channel_id=1, source_target_pairs={{1,0},{2,1},{3,2},{4,3},{5,4},{6,5},{7,6},{8,7},{9,8},{10,9},{11,1... | collective-permute-start | bytes 184328 | tf_op jit(solution)/shard_map/ppermute | solution.py:29
  30.2 7.5 %collective-permute-start.2 = (f32[3,40,4,32]{3,2,1,0:T(4,128)S(1)}, f32[3,40,4,32]{3,2,1,0:T(4,128)S(1)}, u32[]{:S(2)}, u32[]{:S(2)}) collective-permute-start(f32[3,40,4,32]{3,2,1,0:T(4,128)S(1)} %get-tuple-element.365), channel_id=1, source_target_pairs={{0,1},{1,2},{2,3},{3,4},{4,5},{5,6},{6,7},{7,8},{8,9},{9,10},{10,1... | collective-permute-start | bytes 184328 | tf_op jit(solution)/shard_map/ppermute | solution.py:27
  39.8 4.5 copy-start.20
  53.7 0.6 copy-start.8
  53.8 0.7 copy-start.10
  54.6 2.3 copy-start
  58.3 1.2 copy-start.7
  64.5 1.6 copy-start.5
  66.1 3.0 copy-start.3
  71.3 1.6 copy-start.6
  72.8 1.6 copy-start.1
  72.8 2.2 copy-start.2
  76.3 1.0 copy-start.4
  125.2 4.6 copy-start.9
  125.2 4.6 copy-start.11
  183.9 2.2 copy-start.13
  185.7 2.6 copy-start.16
  186.2 3.2 copy-start.21
  186.2 2.6 copy-start.14
  188.8 0.6 copy-start.17
  199.0 0.6 copy-start.8
  199.0 0.7 copy-start.10
  199.9 2.3 copy-start
  203.6 1.2 copy-start.7
  209.8 1.6 copy-start.5
  211.4 3.0 copy-start.3
  216.5 1.6 copy-start.6
  218.1 1.6 copy-start.1
  218.1 2.2 copy-start.2
  221.6 1.0 copy-start.4
  270.3 4.6 copy-start.9
  270.3 4.6 copy-start.11
  329.3 2.2 copy-start.13
  331.1 2.6 copy-start.16
  331.5 3.2 copy-start.21
  331.5 2.6 copy-start.14
  334.1 0.6 copy-start.17
  344.6 7.3 %collective-permute-start.6 = (f32[2,2,3]{2,1,0:T(2,128)S(1)}, f32[2,2,3]{2,1,0:T(2,128)S(1)}, u32[]{:S(2)}, u32[]{:S(2)}) collective-permute-start(f32[2,2,3]{2,1,0:T(2,128)S(1)} %pad_maximum_fusion.19), channel_id=1, source_target_pairs={{0,1},{1,2},{2,3},{3,4},{4,5},{5,6},{6,7},{7,8},{8,9},{9,10},{10,1... | collective-permute-start | bytes 152 | tf_op jit(solution)/shard_map/ppermute | solution.py:17
  351.9 4.6 collective-permute-start.7
  357.3 2.4 collective-permute-start.8
  359.8 8.2 %collective-permute-start.9 = (f32[2,2,3]{2,1,0:T(2,128)S(1)}, f32[2,2,3]{2,1,0:T(2,128)S(1)}, u32[]{:S(2)}, u32[]{:S(2)}) collective-permute-start(f32[2,2,3]{2,1,0:T(2,128)S(1)} %pad_maximum_fusion.20), channel_id=1, source_target_pairs={{0,31},{1,0},{2,1},{3,2},{4,3},{5,4},{6,5},{7,6},{8,7},{9,8},{10,9... | collective-permute-start | bytes 152 | tf_op jit(solution)/shard_map/ppermute | solution.py:17
  369.9 1.2 collective-permute-start.10
  371.2 4.2 collective-permute-start.11
  606.1 2.8 collective-permute-start.12
  608.9 3.1 collective-permute-start.13
  614.0 1.2 collective-permute-start.14
  615.2 4.2 collective-permute-start.15
  701.1 2.7 collective-permute-start.16
  703.8 6.3 collective-permute-start.17
  714.1 1.8 copy-start.15
